TPU v7x, 256 devices: a whole 4x4x8 slice. The times are simulated.
256 devices in a mesh: row: 16 (over x_lo, z), col: 16 (over x_hi, y, core).
Axes of the slice: x: 4 (x_hi: 2, x_lo: 2; x = x_hi * 2 + x_lo), y: 4, z: 8, core: 2. Of those that a mesh axis runs over, the one named last changes fastest.
Arguments:
- adjoints: bfloat16 [4096, 16, 200], P(('row', 'col')), may hold values from -6 to 6
- jac_blocks: bfloat16 [16, 16, 128, 200, 200], P('row', 'col'), may hold values from -0.4375 to 0.4375
- jac_rows: int32 [16, 16, 128], P('row', 'col'), may hold values from 0 to 255, as said below
- jac_cols: int32 [16, 16, 128], P('row', 'col'), may hold values from 0 to 255, as said below
- tile_count: int32 [16, 16], P('row', 'col'), may hold values from 32 to 128, as said below
Outputs:
- transposed: bfloat16 [4096, 16, 200], P('col')
Inputs may be any that keep to these rules, and one draw needn't show every extreme that they name: `jac_rows`: row faces within a tile; both ends are named by some slot. `jac_cols`: column faces within a tile; both ends are named by some slot. `tile_count`: slots at or above the count are padding and are ignored; some tile has exactly 128 live slots.
All inputs are finite; a program needn't handle non-finite values.
Results may differ from a plain program's by a relative error of at most 0.001.
Values may be sent and summed in bfloat16 or wider, within the bound.
No kernel may reach another device: no remote copies, remote signals or barrier semaphores. Data moves between devices by JAX's collectives and lax.ppermute only.
A program may use at most 64 MiB of HBM per device.

v0:
```python
import jax
import jax.numpy as jnp
from jax import lax
from jax.sharding import PartitionSpec as P


def add_columns(selector, products):
    return jnp.einsum(
        "cs,ske->cke",
        selector,
        products,
        preferred_element_type=jnp.float32,
        precision=lax.Precision.HIGHEST,
    )


def on_device(adjoints, jac_blocks, jac_rows, jac_cols, tile_count):
    row_block = lax.all_gather(adjoints, "col", axis=0, tiled=True)
    blocks = jac_blocks[0, 0]
    slot_rows = jac_rows[0, 0]
    slot_cols = jac_cols[0, 0]
    live_count = tile_count[0, 0]
    slot_count = slot_rows.shape[0]
    faces_here = adjoints.shape[0]
    column_count = faces_here * lax.axis_size("row")
    picked = jnp.take(row_block, slot_rows, axis=0)
    products = jnp.einsum("skd,sde->ske", picked, blocks, preferred_element_type=jnp.float32)
    live_slot = jnp.arange(slot_count, dtype=jnp.int32) < live_count
    matches = live_slot[None, :] & (
        slot_cols[None, :] == jnp.arange(column_count, dtype=jnp.int32)[:, None]
    )
    partial_value = add_columns(matches.astype(jnp.float32), products)
    summed = lax.psum(partial_value, "row")
    return summed.astype(jnp.bfloat16)


def solution(mesh):
    placed = (
        P(("row", "col"), None, None),
        P("row", "col", None, None, None),
        P("row", "col", None),
        P("row", "col", None),
        P("row", "col"),
    )
    return jax.shard_map(
        on_device, mesh=mesh, in_specs=placed, out_specs=P("col", None, None), check_vma=False
    )
```

profile of v0, /device:TPU:2, one launch (start us, length us, event | category | flops | bytes accessed | tf_op | source)
XLA Modules:
  0.0 172.7 jit_solution(8518587678829528338)
XLA Ops:
  6.5 0.0 all-gather.2.cloned.1.call-start
  6.5 0.7 all-gather.2.cloned.1.call-update
  7.9 0.0 copy-start.1
  7.9 19.1 %copy.6 = bf16[128,200,200]{2,1,0:T(8,128)(2,1)} copy(bf16[128,200,200]{0,2,1:T(8,128)(2,1)} %bitcast.15) | data formatting | bytes 20480000 | tf_op jit(solution)/shard_map/squeeze | solution.py:19
  27.0 0.0 copy-done.1
  27.1 37.7 %all-gather.2.cloned.1.call-done = bf16[256,16,200]{2,1,0:T(8,128)(2,1)} async-done(((bf16[16,16,200]{2,1,0:T(8,128)(2,1)}), bf16[256,16,200]{2,1,0:T(8,128)(2,1)}) %all-gather.2.cloned.1.call-update) | async-done | bytes 1638416 | tf_op jit(solution)/shard_map/all_gather | solution.py:18
  64.7 2.2 %gather_fusion = bf16[128,16,200]{2,1,0:T(8,128)(2,1)S(1)} fusion(bf16[256,16,200]{2,1,0:T(8,128)(2,1)} %all-gather.2.cloned.1.call-done, s32[1024]{0:T(1024)S(1)} %pad_clamp_fusion), kind=kCustom, calls=%fused_computation | custom fusion | bytes 1638912 | tf_op jit(solution)/shard_map/jit(_take)/gather | solution.py:26
  67.0 6.7 %fusion = f32[128,16,200]{2,1,0:T(8,128)S(1)} fusion(bf16[128,200,200]{2,1,0:T(8,128)(2,1)} %copy.6, bf16[128,16,200]{2,1,0:T(8,128)(2,1)S(1)} %gather_fusion, pred[128]{0:T(512)(128)(4,1)S(1)} %compare_and_fusion), kind=kOutput, calls=%fused_computation.1 | convolution fusion | flops 164249600 | bytes 12697728 | tf_op jit(solution)/shard_map/skd,sde->ske/dot_general | solution.py:27
  73.7 0.0 copy-start
  73.7 1.8 %copy.7 = f32[128,16,200]{0,2,1:T(8,128)} copy(f32[128,16,200]{2,1,0:T(8,128)S(1)} %fusion) | data formatting | bytes 3276800 | tf_op jit(solution)/shard_map/skd,sde->ske/dot_general | solution.py:27
  75.5 0.0 copy-done
  75.5 2.9 %fusion.5 = f32[256,3200]{0,1:S(1)} fusion(f32[128,3200]{0,1:T(8,128)} %bitcast.16, s32[128]{0:T(128)S(1)} %bitcast.17, pred[128]{0:T(512)(128)(4,1)S(1)} %iota_compare_fusion.1), kind=kOutput, calls=%fused_computation.7 | convolution fusion | flops 1258356736 | bytes 4915840
  78.4 87.5 %all-reduce.1 = bf16[256,16,200]{0,2,1:T(8,128)(2,1)} all-reduce(f32[256,16,200]{0,2,1:T(8,128)S(1)} %bitcast.14), channel_id=1, replica_groups=mesh['row'=16,'col'=16] {'row'}, use_global_device_ids=true, to_apply=%region_0.1 | all-reduce | flops 819200 | bytes 4915200 | tf_op jit(solution)/shard_map/psum | solution.py:33
  (4 shorter events, 0.0 us)
Async XLA Ops:
  6.5 58.2 %all-gather.2.cloned.1.call-start = ((), (), s32[]{:S(2)}) async-start(), calls=%async_computation | async-start | bytes 2228224 | tf_op jit(solution)/shard_map/all_gather | solution.py:18
  7.9 19.1 %copy-start.1 = (s32[1,1,128]{2,1,0:T(1,128)S(1)}, s32[1,1,128]{2,1,0:T(1,128)}, u32[]{:S(2)}) copy-start(s32[1,1,128]{2,1,0:T(1,128)} %param.7) | copy-start | bytes 1540
  73.7 1.8 %copy-start = (s32[1,1,128]{2,1,0:T(1,128)S(1)}, s32[1,1,128]{2,1,0:T(1,128)}, u32[]{:S(2)}) copy-start(s32[1,1,128]{2,1,0:T(1,128)} %param.8) | copy-start | bytes 1540
Sparse Core Ops, SparseCore 0:
  10.1 54.6 all-gather.1
where the time goes:
time: 173 us
  blocking collectives  87.5 us (51%)
  waiting for transfers between devices  38.4 us (22%)
  local copies, waits for them, and re-layouts  23.1 us (13%)
  between operations  14.1 us (8%)
  matrix products  9.58 us (6%)
    psum x1, blocking collectives, on_device(): summed = lax.psum(partial_value, 'row')  87.5 us
    all_gather x1, waiting for transfers between devices, on_device(): row_block = lax.all_gather(adjoints, 'col', axis=0, tiled=True)  37.7 us
    squeeze x1, local copies, waits for them, and re-layouts, on_device(): blocks = jac_blocks[0, 0]  19.1 us
    dot_general x1, matrix products, on_device(): jnp.einsum('skd,sde->ske', picked, blocks, preferred_element_type=jnp.flo...  6.7 us
  transfers between devices with their start and end apart: 1, of which 1 were waited for; matrix products, arithmetic and copies ran while one was open for 11% of the time, Pallas kernels for 0%

commit v1 on v0

--- a/solution.py
+++ b/solution.py
@@ -15,7 +15,8 @@
 
 
 def on_device(adjoints, jac_blocks, jac_rows, jac_cols, tile_count):
-    row_block = lax.all_gather(adjoints, "col", axis=0, tiled=True)
+    repeated = jnp.stack([adjoints] * lax.axis_size("col"))
+    row_block = jnp.concatenate(lax.all_to_all(repeated, "col", 0, 0), axis=0)
     blocks = jac_blocks[0, 0]
     slot_rows = jac_rows[0, 0]
     slot_cols = jac_cols[0, 0]

time: 173 us -> 141 us (0.82)
  waiting for transfers between devices: 38.4 us -> 9.94 us
  between operations: 14.1 us -> 0.71 us
  starting transfers between devices: 0.01 us -> 6.14 us
    all_gather x1 -> x0, waiting for transfers between devices: 37.7 us -> none  [on_device(): row_block = lax.all_gather(adjoints, 'col', axis=0, tiled=True)]
    all_to_all x0 -> x1, waiting for transfers between devices: none -> 9.94 us  [on_device(): row_block = jnp.concatenate(lax.all_to_all(repeated, 'col', 0, 0), axis=0)]
    all_to_all x0 -> x1, starting transfers between devices: none -> 6.14 us  [on_device(): row_block = jnp.concatenate(lax.all_to_all(repeated, 'col', 0, 0), axis=0)]
    another operation x0 -> x1, local copies, waits for them, and re-layouts: none -> 2.42 us  [on_device(): repeated = jnp.stack([adjoints] * lax.axis_size('col'))]
  transfers between devices with their start and end apart: 1 -> 1, of which waited for: 1 -> 1; matrix products, arithmetic and copies ran while one was open for 11% -> 14% of each run, Pallas kernels for 0% -> 0%
where the time goes in v1:
time: 141 us; the launch traced here: 139 us
  blocking collectives  88.9 us (63%)
  local copies, waits for them, and re-layouts  24 us (17%)
  waiting for transfers between devices  9.94 us (7%)
  matrix products  9.58 us (7%)
  starting transfers between devices  6.14 us (4%)
    psum x1, blocking collectives, on_device(): summed = lax.psum(partial_value, 'row')  88.9 us
    squeeze x1, local copies, waits for them, and re-layouts, on_device(): blocks = jac_blocks[0, 0]  19.1 us
    all_to_all x1, waiting for transfers between devices, on_device(): row_block = jnp.concatenate(lax.all_to_all(repeated, 'col', 0, 0), axis=0)  9.94 us
    dot_general x1, matrix products, on_device(): jnp.einsum('skd,sde->ske', picked, blocks, preferred_element_type=jnp.flo...  6.7 us
    all_to_all x1, starting transfers between devices, on_device(): row_block = jnp.concatenate(lax.all_to_all(repeated, 'col', 0, 0), axis=0)  6.14 us
    unnamed x1, matrix products  2.89 us
  transfers between devices with their start and end apart: 1, of which 1 were waited for; matrix products, arithmetic and copies ran while one was open for 14% of the time, Pallas kernels for 0%

profile of v1, /device:TPU:2, one launch (start us, length us, event | category | flops | bytes accessed | tf_op | source)
XLA Modules:
  0.0 139.3 jit_solution(16399536258181379346)
XLA Ops:
  0.0 2.4 %stack.2 = bf16[16,16,16,200]{3,2,1,0:T(8,128)(2,1)} broadcast(bf16[16,16,200]{2,1,0:T(8,128)(2,1)} %param.5), dimensions={1,2,3} | broadcast | bytes 1740800 | tf_op jit(solution)/shard_map/stack | solution.py:18
  2.4 6.1 %all-to-all-start = ((bf16[16,16,16,200]{3,2,1,0:T(8,128)(2,1)}), bf16[16,16,16,200]{3,2,1,0:T(8,128)(2,1)S(1)}, u32[]{:S(2)}, u32[]{:S(2)}) async-start(bf16[16,16,16,200]{3,2,1,0:T(8,128)(2,1)} %stack.2), calls=%async_computation | async-start | bytes 4194304 | tf_op jit(solution)/shard_map/all_to_all | solution.py:19
  9.2 0.0 copy-start.1
  9.2 19.1 %copy.6 = bf16[128,200,200]{2,1,0:T(8,128)(2,1)} copy(bf16[128,200,200]{0,2,1:T(8,128)(2,1)} %bitcast.16) | data formatting | bytes 20480000 | tf_op jit(solution)/shard_map/squeeze | solution.py:20
  28.3 0.0 copy-done.1
  28.4 9.9 %all-to-all-done = bf16[16,16,16,200]{3,2,1,0:T(8,128)(2,1)S(1)} async-done(((bf16[16,16,16,200]{3,2,1,0:T(8,128)(2,1)}), bf16[16,16,16,200]{3,2,1,0:T(8,128)(2,1)S(1)}, u32[]{:S(2)}, u32[]{:S(2)}) %all-to-all-start) | async-done | bytes 1638432 | tf_op jit(solution)/shard_map/all_to_all | solution.py:19
  38.3 0.6 gather_fusion
  39.0 6.7 %fusion = f32[128,16,200]{2,1,0:T(8,128)S(1)} fusion(bf16[128,200,200]{2,1,0:T(8,128)(2,1)} %copy.6, bf16[128,16,200]{2,1,0:T(8,128)(2,1)S(1)} %gather_fusion, pred[128]{0:T(512)(128)(4,1)S(1)} %compare_and_fusion), kind=kOutput, calls=%fused_computation.1 | convolution fusion | flops 164249600 | bytes 12697728 | tf_op jit(solution)/shard_map/skd,sde->ske/dot_general | solution.py:28
  45.7 0.0 copy-start
  45.7 1.8 %copy.7 = f32[128,16,200]{0,2,1:T(8,128)} copy(f32[128,16,200]{2,1,0:T(8,128)S(1)} %fusion) | data formatting | bytes 3276800 | tf_op jit(solution)/shard_map/skd,sde->ske/dot_general | solution.py:28
  47.5 0.0 copy-done
  47.5 2.9 %fusion.5 = f32[256,3200]{0,1:S(1)} fusion(f32[128,3200]{0,1:T(8,128)} %bitcast.17, s32[128]{0:T(128)S(1)} %bitcast.19, pred[128]{0:T(512)(128)(4,1)S(1)} %iota_compare_fusion.1), kind=kOutput, calls=%fused_computation.7 | convolution fusion | flops 1258356736 | bytes 4915840
  50.4 88.9 %all-reduce.1 = bf16[256,16,200]{0,2,1:T(8,128)(2,1)} all-reduce(f32[256,16,200]{0,2,1:T(8,128)S(1)} %bitcast.15), channel_id=1, replica_groups=mesh['row'=16,'col'=16] {'row'}, use_global_device_ids=true, to_apply=%region_0.1 | all-reduce | flops 819200 | bytes 4915200 | tf_op jit(solution)/shard_map/psum | solution.py:34
  (4 shorter events, 0.0 us)
Async XLA Ops:
  2.4 35.9 %all-to-all-start = ((bf16[16,16,16,200]{3,2,1,0:T(8,128)(2,1)}), bf16[16,16,16,200]{3,2,1,0:T(8,128)(2,1)S(1)}, u32[]{:S(2)}, u32[]{:S(2)}) async-start(bf16[16,16,16,200]{3,2,1,0:T(8,128)(2,1)} %stack.2), calls=%async_computation | async-start | bytes 4194304 | tf_op jit(solution)/shard_map/all_to_all | solution.py:19
  9.2 19.1 %copy-start.1 = (s32[1,1,128]{2,1,0:T(1,128)S(1)}, s32[1,1,128]{2,1,0:T(1,128)}, u32[]{:S(2)}) copy-start(s32[1,1,128]{2,1,0:T(1,128)} %param.7) | copy-start | bytes 1540
  45.7 1.8 %copy-start = (s32[1,1,128]{2,1,0:T(1,128)S(1)}, s32[1,1,128]{2,1,0:T(1,128)}, u32[]{:S(2)}) copy-start(s32[1,1,128]{2,1,0:T(1,128)} %param.8) | copy-start | bytes 1540
